TPU v7x, 1024 devices: a whole 8x8x8 slice. The times are simulated.
1024 devices in a mesh: pipe: 16 (over z, x_hi), expert: 64 (over x_lo, y, core).
Axes of the slice: x: 8 (x_hi: 2, x_lo: 4; x = x_hi * 4 + x_lo), y: 8, z: 8, core: 2. Of those that a mesh axis runs over, the one named last changes fastest.
Arguments:
- up_state: bfloat16 [16, 1024, 3584], P('pipe', 'expert'), may hold values from -6 to 6
- down_state: bfloat16 [16, 1024, 3584], P('pipe', 'expert'), may hold values from -6 to 6
- entering_up: bfloat16 [1024, 3584], P('expert'), may hold values from -6 to 6
- entering_down: bfloat16 [1024, 3584], P('expert'), may hold values from -6 to 6
- up_route: int32 [2, 16, 1024, 1], P(None, 'pipe', 'expert'), may hold values from 0 to 7; in each aligned block of 16 rows (0 to 15, 16 to 31, ..., all dimensions but the last counted through in order) at most 2 rows name the same one
- down_route: int32 [2, 16, 1024, 1], P(None, 'pipe', 'expert'), may hold values from 0 to 7; in each aligned block of 16 rows (0 to 15, 16 to 31, ..., all dimensions but the last counted through in order) at most 2 rows name the same one
- norm_gain: float32 [16, 3584], P('pipe'), may hold values from 0.5 to 1.5
- router: bfloat16 [16, 3584, 8], P('pipe'), may hold values from -0.09375 to 0.09375
- w_gate: bfloat16 [16, 3584, 8192], P('pipe', None, 'expert'), may hold values from -0.09375 to 0.09375
- w_up: bfloat16 [16, 3584, 8192], P('pipe', None, 'expert'), may hold values from -0.09375 to 0.09375
- w_down: bfloat16 [16, 8192, 3584], P('pipe', 'expert'), may hold values from -0.1875 to 0.1875
Outputs:
- up_out: bfloat16 [16, 1024, 3584], P('pipe', 'expert')
- down_out: bfloat16 [16, 1024, 3584], P('pipe', 'expert')
Inputs may be any that keep to these rules, and one draw needn't show every extreme that they name: `up_route`: each row names one expert. Within each aligned block of 16 rows (the rows of one device) every expert is named by exactly 2 rows. `down_route`: as for up_route.
All inputs are finite; a program needn't handle non-finite values.
Results may differ from a plain program's by a relative error of at most 0.0057.
Values may be sent and summed in bfloat16 or wider, within the bound.
A program may use at most 32 MiB of HBM per device.

v0:
```python
import jax
import jax.numpy as jnp
from jax import lax
from jax.sharding import PartitionSpec as P

TOP = 1
TICKS = 2


norm_eps = 1e-06


def shifted(value, axis, by):
    length = lax.axis_size(axis)
    pairs = [(i, i + by) for i in range(length) if 0 <= i + by < length]
    return lax.ppermute(value, axis, pairs)


def normalize(token_rows, gain_row):
    widened = token_rows.astype(jnp.float32)
    inverse = lax.rsqrt(jnp.mean(widened * widened, axis=1, keepdims=True) + norm_eps)
    return (widened * inverse * gain_row).astype(jnp.bfloat16)


def routing_tables(normed, routing, router_cols, expert_count, slot_cap):
    logits = jnp.dot(normed, router_cols, preferred_element_type=jnp.float32)
    affinity = jax.nn.sigmoid(logits)
    weights = jnp.take_along_axis(affinity, routing, axis=1)
    flat_ids = routing.reshape(-1)
    onehot = (flat_ids[:, None] == jnp.arange(expert_count, dtype=jnp.int32)[None, :]).astype(
        jnp.int32
    )
    before = jnp.cumsum(onehot, axis=0) - onehot
    slot_ids = jnp.sum(before * onehot, axis=1).reshape(routing.shape)
    expert_hit = (
        routing[:, :, None] == jnp.arange(expert_count, dtype=jnp.int32)[None, None, :]
    ).astype(jnp.float32)
    slot_hit = (
        slot_ids[:, :, None] == jnp.arange(slot_cap, dtype=jnp.int32)[None, None, :]
    ).astype(jnp.float32)
    scatter_map = jnp.einsum("rke,rkc->ecr", expert_hit, slot_hit).astype(jnp.bfloat16)
    flat_slot = routing * slot_cap + slot_ids
    return (scatter_map, weights, flat_slot)


def run_experts(received, gate_cols, up_cols, down_rows):
    sources, slot_count, features = received.shape
    flat_rows = received.reshape(sources * slot_count, features)
    gate_pre = jnp.dot(flat_rows, gate_cols, preferred_element_type=jnp.float32)
    up_pre = jnp.dot(flat_rows, up_cols, preferred_element_type=jnp.float32)
    hidden = (jax.nn.silu(gate_pre) * up_pre).astype(jnp.bfloat16)
    partial_value = jnp.dot(hidden, down_rows, preferred_element_type=jnp.float32).astype(
        jnp.bfloat16
    )
    partial_value = partial_value.reshape(sources, slot_count, features)
    return lax.all_to_all(partial_value, "expert", split_axis=0, concat_axis=0, tiled=True)


def mix_rows(token_rows, weights, flat_slot, outputs):
    picked = outputs[flat_slot]
    return token_rows.astype(jnp.float32) + jnp.sum(weights[:, :, None] * picked, axis=1)


def shards(
    up_state,
    down_state,
    entering_up,
    entering_down,
    up_route,
    down_route,
    norm_gain,
    router,
    w_gate,
    w_up,
    w_down,
):
    gate_cols = w_gate[0]
    up_cols = w_up[0]
    down_rows = w_down[0]
    gain_row = norm_gain[0]
    router_cols = router[0]
    group_size = max(1, lax.axis_size("expert") // 8)
    expert_count = lax.axis_size("expert") // group_size
    segment_id = lax.axis_index("pipe")
    last_segment = lax.axis_size("pipe") - 1
    up_now = up_state[0]
    down_now = down_state[0]
    features = up_now.shape[1]
    slot_cap = up_now.shape[0] * TOP // expert_count
    up_done = up_now
    down_done = down_now
    for tick_id in range(TICKS):
        up_normed = normalize(up_now, gain_row)
        down_normed = normalize(down_now, gain_row)
        up_scatter, up_weights, up_slot = routing_tables(
            up_normed, up_route[tick_id, 0], router_cols, expert_count, slot_cap
        )
        down_scatter, down_weights, down_slot = routing_tables(
            down_normed, down_route[tick_id, 0], router_cols, expert_count, slot_cap
        )
        up_send = jnp.einsum(
            "ecr,rd->ecd", up_scatter, up_normed, preferred_element_type=jnp.float32
        ).astype(jnp.bfloat16)
        down_send = jnp.einsum(
            "ecr,rd->ecd", down_scatter, down_normed, preferred_element_type=jnp.float32
        ).astype(jnp.bfloat16)
        outbound = jnp.concatenate([up_send, down_send], axis=1)
        outgoing = jnp.broadcast_to(
            outbound[:, None], (expert_count, group_size, 2 * slot_cap, features)
        ).reshape(expert_count * group_size, 2 * slot_cap, features)
        returned = run_experts(
            lax.all_to_all(outgoing, "expert", split_axis=0, concat_axis=0, tiled=True),
            gate_cols,
            up_cols,
            down_rows,
        )
        summed = jnp.sum(
            returned.reshape(expert_count, group_size, 2 * slot_cap, features).astype(jnp.float32),
            axis=1,
        )
        up_outputs = summed[:, :slot_cap].reshape(expert_count * slot_cap, features)
        down_outputs = summed[:, slot_cap:].reshape(expert_count * slot_cap, features)
        up_done = mix_rows(up_now, up_weights, up_slot, up_outputs).astype(jnp.bfloat16)
        down_done = mix_rows(down_now, down_weights, down_slot, down_outputs).astype(jnp.bfloat16)
        if tick_id + 1 < TICKS:
            up_moved = shifted(up_done, "pipe", 1)
            down_moved = shifted(down_done, "pipe", -1)
            up_now = jnp.where(segment_id == 0, entering_up, up_moved)
            down_now = jnp.where(segment_id == last_segment, entering_down, down_moved)
    return (up_done[None], down_done[None])


def solution(mesh):
    return jax.shard_map(
        shards,
        mesh=mesh,
        in_specs=(
            P("pipe", "expert", None),
            P("pipe", "expert", None),
            P("expert", None),
            P("expert", None),
            P(None, "pipe", "expert", None),
            P(None, "pipe", "expert", None),
            P("pipe", None),
            P("pipe", None, None),
            P("pipe", None, "expert"),
            P("pipe", None, "expert"),
            P("pipe", "expert", None),
        ),
        out_specs=(P("pipe", "expert", None), P("pipe", "expert", None)),
        check_vma=False,
    )
```

profile of v0, /device:TPU:398, one launch (start us, length us, event | category | flops | bytes accessed | tf_op | source)
XLA Modules:
  0.0 292.1 jit_solution(14246034062872149856)
XLA Ops:
  0.6 1.1 fusion.30
  1.8 1.0 fusion.36
  2.8 0.7 slice_bitcast_fusion.1
  3.5 0.7 slice_bitcast_fusion
  4.2 0.1 fusion.91
  4.3 0.1 fusion.95
  4.4 0.2 select_reduce_fusion
  4.6 0.1 copy.20
  4.7 0.1 fusion.93
  4.8 0.1 fusion.97
  4.9 0.2 select_reduce_fusion.1
  5.2 0.8 reduce
  5.9 1.1 convolution_convert_fusion.5
  7.0 1.1 convolution_convert_fusion.4
  8.2 0.1 copy.21
  8.3 0.5 broadcast_in_dim.8
  8.8 57.9 %all_to_all.20 = bf16[64,4,3584]{2,1,0:T(4,128)(2,1)} all-to-all(bf16[64,4,3584]{2,1,0:T(4,128)(2,1)S(1)} %bitcast.222), channel_id=1, replica_groups=mesh['pipe'=16,'expert'=64] {'expert'}, dimensions={0} | all-to-all | bytes 3670016 | tf_op jit(solution)/shard_map/all_to_all | solution.py:112
  66.7 2.9 %reshape.451 = bf16[256,3584]{1,0:T(8,128)(2,1)S(1)} reshape(bf16[64,4,3584]{2,1,0:T(4,128)(2,1)} %all_to_all.20) | data formatting | bytes 3670016 | tf_op jit(solution)/shard_map/reshape | solution.py:48
  69.6 1.8 fusion.22
  71.4 3.6 %convolution_convert_fusion.1 = bf16[256,3584]{1,0:T(8,128)(2,1)} fusion(bf16[256,3584]{1,0:T(8,128)(2,1)S(1)} %reshape.451, bf16[1,128,3584]{2,1,0:T(8,128)(2,1)S(1)} %copy-done, bf16[1,3584,128]{2,1,0:T(8,128)(2,1)} %param.22, f32[256,128]{1,0:T(8,128)S(1)} %fusion.22), kind=kOutput, calls=%fused_computation.9 | convolution fusion | flops 470876160 | bytes 5636096 | tf_op jit(solution)/shard_map/dot_general | solution.py:52
  75.1 4.1 %reshape.452 = bf16[64,4,3584]{2,1,0:T(4,128)(2,1)} reshape(bf16[256,3584]{1,0:T(8,128)(2,1)} %convolution_convert_fusion.1) | data formatting | bytes 3670016 | tf_op jit(solution)/shard_map/reshape | solution.py:55
  79.1 10.3 %all-to-all-start.1 = ((bf16[64,4,3584]{2,1,0:T(4,128)(2,1)}), bf16[64,4,3584]{2,1,0:T(4,128)(2,1)S(1)}, u32[]{:S(2)}, u32[]{:S(2)}) async-start(bf16[64,4,3584]{2,1,0:T(4,128)(2,1)} %reshape.452), calls=%async_computation.1 | async-start | bytes 3670016 | tf_op jit(solution)/shard_map/all_to_all | solution.py:56
  89.6 0.2 fusion.7
  89.9 0.7 gather_fusion.6
  90.6 0.2 fusion.13
  90.8 0.7 gather_fusion.4
  91.5 44.4 %all-to-all-done.1 = bf16[64,4,3584]{2,1,0:T(4,128)(2,1)S(1)} async-done(((bf16[64,4,3584]{2,1,0:T(4,128)(2,1)}), bf16[64,4,3584]{2,1,0:T(4,128)(2,1)S(1)}, u32[]{:S(2)}, u32[]{:S(2)}) %all-to-all-start.1) | async-done | bytes 1835040 | tf_op jit(solution)/shard_map/all_to_all | solution.py:56
  135.9 0.8 convert_reduce_fusion.1
  136.7 0.2 fusion.133
  136.9 0.2 reshape.453
  137.1 0.6 gather_fusion
  137.7 0.1 fusion.33
  137.8 8.8 %collective-permute-start = (bf16[16,3584]{1,0:T(8,128)(2,1)S(1)}, bf16[16,3584]{1,0:T(8,128)(2,1)S(1)}, u32[]{:S(2)}, u32[]{:S(2)}) collective-permute-start(bf16[16,3584]{1,0:T(8,128)(2,1)S(1)} %fusion.33), channel_id=1, source_target_pairs={{0,64},{64,128},{128,192},{192,256},{256,320},{320,384},{384,448},... | collective-permute-start | bytes 344072 | tf_op jit(solution)/shard_map/ppermute | solution.py:16
  146.6 0.2 reshape.454
  146.8 0.6 gather_fusion.1
  147.5 0.1 fusion.39
  147.6 1.9 collective-permute-start.1
  149.5 2.6 collective-permute-done
  152.1 0.2 fusion.42
  152.2 9.5 %collective-permute-done.1 = bf16[16,3584]{1,0:T(8,128)(2,1)S(1)} collective-permute-done((bf16[16,3584]{1,0:T(8,128)(2,1)S(1)}, bf16[16,3584]{1,0:T(8,128)(2,1)S(1)}, u32[]{:S(2)}, u32[]{:S(2)}) %collective-permute-start.1) | collective-permute-done | bytes 114720 | tf_op jit(solution)/shard_map/ppermute | solution.py:16
  161.8 0.2 fusion.46
  162.0 0.2 convolution_convert_fusion.3
  162.2 0.2 convolution_convert_fusion.2
  162.5 0.1 copy.24
  162.6 0.5 broadcast_in_dim.9
  163.1 56.2 %all_to_all.21 = bf16[64,4,3584]{2,1,0:T(4,128)(2,1)} all-to-all(bf16[64,4,3584]{2,1,0:T(4,128)(2,1)S(1)} %bitcast.223), channel_id=1, replica_groups=mesh['pipe'=16,'expert'=64] {'expert'}, dimensions={0} | all-to-all | bytes 3670016 | tf_op jit(solution)/shard_map/all_to_all | solution.py:112
  219.3 2.9 %reshape.456 = bf16[256,3584]{1,0:T(8,128)(2,1)S(1)} reshape(bf16[64,4,3584]{2,1,0:T(4,128)(2,1)} %all_to_all.21) | data formatting | bytes 3670016 | tf_op jit(solution)/shard_map/reshape | solution.py:48
  222.2 1.8 fusion.20
  224.0 3.6 %convolution_convert_fusion = bf16[256,3584]{1,0:T(8,128)(2,1)} fusion(bf16[256,3584]{1,0:T(8,128)(2,1)S(1)} %reshape.456, bf16[1,128,3584]{2,1,0:T(8,128)(2,1)S(1)} %copy-done, bf16[1,3584,128]{2,1,0:T(8,128)(2,1)} %param.22, f32[256,128]{1,0:T(8,128)S(1)} %fusion.20), kind=kOutput, calls=%fused_computation.8 | convolution fusion | flops 470876160 | bytes 5636096 | tf_op jit(solution)/shard_map/dot_general | solution.py:52
  227.7 4.1 %reshape.457 = bf16[64,4,3584]{2,1,0:T(4,128)(2,1)} reshape(bf16[256,3584]{1,0:T(8,128)(2,1)} %convolution_convert_fusion) | data formatting | bytes 3670016 | tf_op jit(solution)/shard_map/reshape | solution.py:55
  231.7 9.7 %all-to-all-start.3 = ((bf16[64,4,3584]{2,1,0:T(4,128)(2,1)}), bf16[64,4,3584]{2,1,0:T(4,128)(2,1)S(1)}, u32[]{:S(2)}, u32[]{:S(2)}) async-start(bf16[64,4,3584]{2,1,0:T(4,128)(2,1)} %reshape.457), calls=%async_computation.3 | async-start | bytes 3670016 | tf_op jit(solution)/shard_map/all_to_all | solution.py:56
  241.5 0.2 fusion.10
  241.7 0.7 gather_fusion.5
  242.4 0.2 fusion.4
  242.6 0.7 gather_fusion.7
  243.3 44.7 %all-to-all-done.3 = bf16[64,4,3584]{2,1,0:T(4,128)(2,1)S(1)} async-done(((bf16[64,4,3584]{2,1,0:T(4,128)(2,1)}), bf16[64,4,3584]{2,1,0:T(4,128)(2,1)S(1)}, u32[]{:S(2)}, u32[]{:S(2)}) %all-to-all-start.3) | async-done | bytes 1835040 | tf_op jit(solution)/shard_map/all_to_all | solution.py:56
  288.0 0.8 convert_reduce_fusion
  288.8 0.2 fusion.132
  289.0 0.2 reshape.459
  289.1 0.2 reshape.458
  289.3 0.6 gather_fusion.3
  289.9 0.7 fusion.60
  290.7 0.6 gather_fusion.2
  291.3 0.7 fusion.61
  (49 shorter events, 0.6 us)
Async XLA Ops:
  0.6 70.8 %copy-start = (bf16[1,128,3584]{2,1,0:T(8,128)(2,1)S(1)}, bf16[1,128,3584]{2,1,0:T(8,128)(2,1)}, u32[]{:S(2)}) copy-start(bf16[1,128,3584]{2,1,0:T(8,128)(2,1)} %param.23) | copy-start | bytes 2752516
  79.1 10.4 %copy-start.5 = (s32[2,1,16,1]{2,3,1,0:T(1,128)S(1)}, s32[2,1,16,1]{2,3,1,0:T(1,128)}, u32[]{:S(2)}) copy-start(s32[2,1,16,1]{2,3,1,0:T(1,128)} %param.17) | copy-start | bytes 388
  79.1 10.4 %copy-start.6 = (s32[2,1,16,1]{2,3,1,0:T(1,128)S(1)}, s32[2,1,16,1]{2,3,1,0:T(1,128)}, u32[]{:S(2)}) copy-start(s32[2,1,16,1]{2,3,1,0:T(1,128)} %param.18) | copy-start | bytes 388
  79.1 10.5 %copy-start.2 = (bf16[1,16,3584]{2,1,0:T(8,128)(2,1)S(1)}, bf16[1,16,3584]{2,1,0:T(8,128)(2,1)}, u32[]{:S(2)}) copy-start(bf16[1,16,3584]{2,1,0:T(8,128)(2,1)} %param.14) | copy-start | bytes 344068
  79.1 10.5 %copy-start.7 = (bf16[1,3584,8]{1,2,0:T(8,128)(2,1)S(1)}, bf16[1,3584,8]{1,2,0:T(8,128)(2,1)}, u32[]{:S(2)}) copy-start(bf16[1,3584,8]{1,2,0:T(8,128)(2,1)} %param.20) | copy-start | bytes 172036
  79.1 11.4 %copy-start.1 = (bf16[1,16,3584]{2,1,0:T(8,128)(2,1)S(1)}, bf16[1,16,3584]{2,1,0:T(8,128)(2,1)}, u32[]{:S(2)}) copy-start(bf16[1,16,3584]{2,1,0:T(8,128)(2,1)} %param.13) | copy-start | bytes 344068
  79.1 56.8 %all-to-all-start.1 = ((bf16[64,4,3584]{2,1,0:T(4,128)(2,1)}), bf16[64,4,3584]{2,1,0:T(4,128)(2,1)S(1)}, u32[]{:S(2)}, u32[]{:S(2)}) async-start(bf16[64,4,3584]{2,1,0:T(4,128)(2,1)} %reshape.452), calls=%async_computation.1 | async-start | bytes 3670016 | tf_op jit(solution)/shard_map/all_to_all | solution.py:56
  137.7 14.4 %copy-start.3 = (bf16[16,3584]{1,0:T(8,128)(2,1)S(1)}, bf16[16,3584]{1,0:T(8,128)(2,1)}, u32[]{:S(2)}) copy-start(bf16[16,3584]{1,0:T(8,128)(2,1)} %param.15) | copy-start | bytes 344068
  137.7 24.1 %copy-start.4 = (bf16[16,3584]{1,0:T(8,128)(2,1)S(1)}, bf16[16,3584]{1,0:T(8,128)(2,1)}, u32[]{:S(2)}) copy-start(bf16[16,3584]{1,0:T(8,128)(2,1)} %param.16) | copy-start | bytes 344068
  137.8 14.2 %collective-permute-start = (bf16[16,3584]{1,0:T(8,128)(2,1)S(1)}, bf16[16,3584]{1,0:T(8,128)(2,1)S(1)}, u32[]{:S(2)}, u32[]{:S(2)}) collective-permute-start(bf16[16,3584]{1,0:T(8,128)(2,1)S(1)} %fusion.33), channel_id=1, source_target_pairs={{0,64},{64,128},{128,192},{192,256},{256,320},{320,384},{384,448},... | collective-permute-start | bytes 344072 | tf_op jit(solution)/shard_map/ppermute | solution.py:16
  147.6 14.2 %collective-permute-start.1 = (bf16[16,3584]{1,0:T(8,128)(2,1)S(1)}, bf16[16,3584]{1,0:T(8,128)(2,1)S(1)}, u32[]{:S(2)}, u32[]{:S(2)}) collective-permute-start(bf16[16,3584]{1,0:T(8,128)(2,1)S(1)} %fusion.39), channel_id=1, source_target_pairs={{64,0},{128,64},{192,128},{256,192},{320,256},{384,320},{448,384},... | collective-permute-start | bytes 344072 | tf_op jit(solution)/shard_map/ppermute | solution.py:16
  231.7 56.3 %all-to-all-start.3 = ((bf16[64,4,3584]{2,1,0:T(4,128)(2,1)}), bf16[64,4,3584]{2,1,0:T(4,128)(2,1)S(1)}, u32[]{:S(2)}, u32[]{:S(2)}) async-start(bf16[64,4,3584]{2,1,0:T(4,128)(2,1)} %reshape.457), calls=%async_computation.3 | async-start | bytes 3670016 | tf_op jit(solution)/shard_map/all_to_all | solution.py:56
where the time goes:
time: 293 us; the launch traced here: 292 us
  blocking collectives  114 us (39%)
  waiting for transfers between devices  101 us (34%)
  starting transfers between devices  30.7 us (10%)
  local copies, waits for them, and re-layouts  23 us (8%)
  matrix products  14.5 us (5%)
  other arithmetic  7.45 us (3%)
    all_to_all x2, blocking collectives, shards(): lax.all_to_all(outgoing, 'expert', split_axis=0, concat_axis=0, tiled=True)  114 us
    all_to_all x2, waiting for transfers between devices, run_experts(): lax.all_to_all(partial_value, 'expert', split_axis=0, concat_axis=0, tile...  89.1 us
    all_to_all x2, starting transfers between devices, run_experts(): lax.all_to_all(partial_value, 'expert', split_axis=0, concat_axis=0, tile...  20 us
    ppermute x2, waiting for transfers between devices, shifted(): return lax.ppermute(value, axis, pairs)  12.1 us
    ppermute x2, starting transfers between devices, shifted(): return lax.ppermute(value, axis, pairs)  10.7 us
    reshape x2, local copies, waits for them, and re-layouts, run_experts(): partial_value = partial_value.reshape(sources, slot_count, features)  8.11 us
    dot_general x2, matrix products, run_experts(): jnp.dot(hidden, down_rows, preferred_element_type=jnp.float32)  7.25 us
    reshape x2, local copies, waits for them, and re-layouts, run_experts(): flat_rows = received.reshape(sources * slot_count, features)  5.87 us
  transfers between devices with their start and end apart: 4, of which 4 were waited for; matrix products, arithmetic and copies ran while one was open for 2% of the time, Pallas kernels for 0%

commit v1 on v0

v1 whole, which is shorter than its diff:
```python
import functools

import jax
import jax.numpy as jnp
from jax import lax
from jax.experimental import pallas as pl
from jax.experimental.pallas import tpu as pltpu
from jax.sharding import PartitionSpec as P

XS, YS, CORES = 4, 8, 2
HALF = YS // 2
TICKS = 2
ROWS = 16
SLOTS = 8
PARTS = 4
REACH = 5
TRANSIT = 5
norm_eps = 1e-06

MESH = pl.DeviceIdType.MESH
F32, BF16 = jnp.float32, jnp.bfloat16


def iota(shape, dim):
    return lax.broadcasted_iota(jnp.int32, shape, dim)


def turned(row):
    n = row.shape[1]
    eye = iota((n, n), 0) == iota((n, n), 1)
    return jnp.sum(jnp.where(eye, jnp.broadcast_to(row, (n, n)), 0.0), axis=1, keepdims=True)


def slots_of(route, direction):
    n = route.shape[1]
    column = turned(route)
    earlier = iota((n, n), 0) < iota((n, n), 1)
    same = (jnp.broadcast_to(column, (n, n)) == jnp.broadcast_to(route, (n, n))) & earlier
    number = jnp.sum(jnp.where(same, 1.0, 0.0), axis=0, keepdims=True)
    return route * 4.0 + (2.0 * direction) + number


def kernel(
    pipes,
    up_ref, down_ref, enter_up_ref, enter_down_ref, up_route_ref, down_route_ref,
    gain_ref, router_ref, w_gate_ref, w_up_ref, w_down_ref,
    up_out_ref, down_out_ref,
    wgu, wd, normed, xsend, xrecv, away, blocks, pass_on, part, csend, crecv, bsend, brecv, moved_out, moved,
    w_local, w_send, w_recv, x_send, x_recv, y_send, y_recv, c_send, c_recv, b_send, b_recv, m_send, m_recv,
):
    features = up_ref.shape[1]
    width = features // PARTS
    hid = w_down_ref.shape[0]
    pipe = lax.axis_index("pipe")
    place = lax.axis_index("expert")
    core = lax.rem(place, CORES)
    y = lax.rem(place // CORES, YS)
    x = place // (CORES * YS)
    half = y // HALF
    j = lax.rem(y, HALF)

    def at(xx, yy, cc):
        return (pipe, (xx * YS + yy) * CORES + cc)

    def chunk(f):
        return pl.ds(f * width, width)

    def remote(src, dst, send, recv, device):
        return pltpu.make_async_remote_copy(
            src_ref=src, dst_ref=dst, send_sem=send, recv_sem=recv, device_id=device, device_id_type=MESH
        )

    sibling = at(x, y, 1 - core)
    nexts = (at(x, lax.rem(y + 1, YS), core), at(x, lax.rem(y + YS - 1, YS), core))
    ahead = (lax.rem(pipe + 1, pipes), place)
    behind = (lax.rem(pipe + pipes - 1, pipes), place)
    shifts = (ahead, behind)

    def toward(direction, d):
        return lax.rem(y + (d if direction == 0 else YS - d), YS)

    def back(direction, d):
        return toward(1 - direction, d)

    rank = (j, HALF - 1 - j)

    own_weights = [
        pltpu.make_async_copy(w_gate_ref, wgu.at[:, pl.ds(0, hid)], w_local.at[0]),
        pltpu.make_async_copy(w_up_ref, wgu.at[:, pl.ds(2 * hid, hid)], w_local.at[1]),
        pltpu.make_async_copy(w_down_ref, wd.at[pl.ds(0, hid), :], w_local.at[2]),
    ]
    for copy in own_weights:
        copy.start()

    barrier = pltpu.get_barrier_semaphore()
    partners = [at(lax.rem(x + i, XS), y, core) for i in range(1, XS)] + [*nexts, sibling, *shifts]
    for device in partners:
        pl.semaphore_signal(barrier, inc=1, device_id=device, device_id_type=MESH)

    sent = []

    def prepare(t, sources):
        tables = []
        picks = []
        for direction, (source, route_ref) in enumerate(zip(sources, (up_route_ref, down_route_ref))):
            rows = source[...].astype(F32)
            inverse = lax.rsqrt(jnp.mean(rows * rows, axis=1, keepdims=True) + norm_eps)
            normed[direction] = (rows * inverse * gain_ref[...]).astype(BF16)
            route = route_ref[pl.ds(t, 1), :].astype(F32)
            spot = slots_of(route, direction)
            pick = (iota((2 * ROWS, ROWS), 0).astype(F32) == jnp.broadcast_to(spot, (2 * ROWS, ROWS))).astype(BF16)
            picks.append(pick)
            tables.append((route, spot))
        return tables, picks

    def send_rows(t, picks):
        for f in range(PARTS):
            rows = jnp.dot(picks[0], normed[0, :, chunk(f)], preferred_element_type=F32) + jnp.dot(
                picks[1], normed[1, :, chunk(f)], preferred_element_type=F32
            )
            xsend[t, :, :, chunk(f)] = rows.reshape(XS, SLOTS, width).astype(BF16)
        if t == 0:
            pl.semaphore_wait(barrier, len(partners))
        for f in range(PARTS):
            for i in range(1, XS):
                target = lax.rem(x + i, XS)
                copy = remote(
                    xsend.at[t, target, :, chunk(f)], xrecv.at[t, x, :, chunk(f)],
                    x_send.at[t, i - 1, f], x_recv.at[t, i - 1, f], at(target, y, core),
                )
                copy.start()
                sent.append((None, copy))
        xrecv[t, pl.ds(x, 1)] = xsend[t, pl.ds(x, 1)]

    def weigh(t, tables):
        out = []
        for direction, (route, spot) in enumerate(tables):
            logits = lax.dot_general(
                router_ref[...], normed[direction], (((1,), (1,)), ((), ())), preferred_element_type=F32
            )
            affinity = jax.nn.sigmoid(logits)
            count = affinity.shape[0]
            hit = iota((count, ROWS), 0).astype(F32) == jnp.broadcast_to(route, (count, ROWS))
            weight = jnp.sum(jnp.where(hit, affinity, 0.0), axis=0, keepdims=True)
            undo = (iota((ROWS, 2 * ROWS), 1).astype(F32) == jnp.broadcast_to(turned(spot), (ROWS, 2 * ROWS))).astype(BF16)
            out.append((turned(weight), undo))
        return out

    def regroup(back_again):
        a, b = iota((2 * ROWS, 2 * ROWS), 0), iota((2 * ROWS, 2 * ROWS), 1)
        if back_again:
            a, b = b, a
        want = lax.rem(a // 4, XS) * SLOTS + (a // ROWS) * 4 + lax.rem(a, 4)
        return (want == b).astype(BF16)

    def remember(when, copy):
        sent.append((when, copy))

    def guarded(condition, make):
        copy = make()

        @pl.when(condition)
        def _():
            copy.start()

        remember(condition, copy)

    def spread(t):
        forward = regroup(False)
        for f in range(PARTS):
            for i in range(1, XS):
                remote(
                    xsend.at[t, 0, :, chunk(f)], xrecv.at[t, 0, :, chunk(f)],
                    x_send.at[t, i - 1, f], x_recv.at[t, i - 1, f], sibling,
                ).wait_recv()
            rows = xrecv[t, :, :, chunk(f)].astype(F32).reshape(2 * ROWS, width).astype(BF16)
            rows = jnp.dot(forward, rows, preferred_element_type=F32)
            low, high = rows[:ROWS], rows[ROWS:]
            first = half == 0
            blocks[t, pl.ds(y, 1), :, chunk(f)] = jnp.where(first, low, high).astype(BF16)[None]
            away[t, :, chunk(f)] = jnp.where(first, high, low).astype(BF16)
            for r in range(2):
                k = rank[r]
                guarded(k == HALF - 2, lambda: remote(
                    away.at[t, :, chunk(f)], pass_on.at[t, r, :, chunk(f)],
                    y_send.at[t, r, TRANSIT, f], y_recv.at[t, r, TRANSIT, f], nexts[r],
                ))
                guarded(k == HALF - 1, lambda: remote(
                    away.at[t, :, chunk(f)], blocks.at[t, y, :, chunk(f)],
                    y_send.at[t, r, 0, f], y_recv.at[t, r, 0, f], nexts[r],
                ))
            for r in range(2):
                k = rank[r]
                guarded(k < HALF - 1, lambda: remote(
                    blocks.at[t, y, :, chunk(f)], blocks.at[t, y, :, chunk(f)],
                    y_send.at[t, r, 0, f], y_recv.at[t, r, 0, f], nexts[r],
                ))
        for f in range(PARTS):
            for r in range(2):
                k = rank[r]

                @pl.when(k == HALF - 1)
                def _():
                    remote(
                        pass_on.at[t, r, :, chunk(f)], pass_on.at[t, r, :, chunk(f)],
                        y_send.at[t, r, TRANSIT, f], y_recv.at[t, r, TRANSIT, f], nexts[r],
                    ).wait_recv()

                guarded(k == HALF - 1, lambda: remote(
                    pass_on.at[t, r, :, chunk(f)], blocks.at[t, back(r, 1), :, chunk(f)],
                    y_send.at[t, r, 1, f], y_recv.at[t, r, 1, f], nexts[r],
                ))
        for d in range(1, REACH + 1):
            for f in range(PARTS):
                for r in range(2):
                    k = rank[r]
                    slot = back(r, d)

                    @pl.when(d <= k + 2)
                    def _():
                        remote(
                            blocks.at[t, slot, :, chunk(f)], blocks.at[t, slot, :, chunk(f)],
                            y_send.at[t, r, d - 1, f], y_recv.at[t, r, d - 1, f], nexts[r],
                        ).wait_recv()

                    if d < REACH:
                        guarded((k < HALF - 1) & (d <= k + 2), lambda: remote(
                            blocks.at[t, slot, :, chunk(f)], blocks.at[t, slot, :, chunk(f)],
                            y_send.at[t, r, d, f], y_recv.at[t, r, d, f], nexts[r],
                        ))

    def experts(t):
        total = jnp.zeros((YS * ROWS, 4 * hid), F32)
        for f in range(PARTS):
            total = total + jnp.dot(
                blocks[t, :, :, chunk(f)].reshape(YS * ROWS, width), wgu[chunk(f), :], preferred_element_type=F32
            )
        gate, up = total[:, : 2 * hid], total[:, 2 * hid :]
        hidden = (gate / (1.0 + jnp.exp(-gate)) * up).astype(BF16)
        for f in range(PARTS):
            piece = jnp.dot(hidden, wd[:, chunk(f)], preferred_element_type=F32)
            part[:, :, chunk(f)] = piece.reshape(YS, ROWS, width)

    def gather(t):
        for d in range(REACH, 0, -1):
            for f in range(PARTS):
                for r in range(2):
                    k = rank[r]
                    slot = toward(r, d)

                    @pl.when(k == 0)
                    def _():
                        csend[t, r, d - 1, :, chunk(f)] = part[slot, :, chunk(f)].astype(BF16)

                    if d < REACH:

                        @pl.when((k >= 1) & (d <= REACH - k))
                        def _():
                            remote(
                                csend.at[t, r, d - 1, :, chunk(f)], crecv.at[t, r, d, :, chunk(f)],
                                c_send.at[t, r, d - 1, f], c_recv.at[t, r, d, f], nexts[r],
                            ).wait_recv()
                            both = part[slot, :, chunk(f)] + crecv[t, r, d, :, chunk(f)].astype(F32)
                            csend[t, r, d - 1, :, chunk(f)] = both.astype(BF16)

                    guarded((k < HALF - 1) & (d <= REACH - k), lambda: remote(
                        csend.at[t, r, d - 1, :, chunk(f)], crecv.at[t, r, d - 1, :, chunk(f)],
                        c_send.at[t, r, d - 1, f], c_recv.at[t, r, d - 1, f], nexts[r],
                    ))
                    if d <= 2:
                        guarded(k == HALF - 1, lambda: remote(
                            csend.at[t, r, d - 1, :, chunk(f)], crecv.at[t, r, 6 - d, :, chunk(f)],
                            c_send.at[t, r, d - 1, f], c_recv.at[t, r, 6 - d, f], nexts[r],
                        ))

        def arrival(r, slot, f):
            return remote(
                csend.at[t, r, 0, :, chunk(f)], crecv.at[t, r, slot, :, chunk(f)],
                c_send.at[t, r, 0, f], c_recv.at[t, r, slot, f], nexts[r],
            )

        for f in range(PARTS):
            for r in range(2):
                k = rank[r]

                @pl.when(k == 0)
                def _():
                    arrival(r, 4, f).wait_recv()

                guarded(k == 0, lambda: remote(
                    crecv.at[t, r, 4, :, chunk(f)], crecv.at[t, r, TRANSIT, :, chunk(f)],
                    c_send.at[t, r, TRANSIT, f], c_recv.at[t, r, TRANSIT, f], nexts[r],
                ))
        backward = regroup(True)
        for f in range(PARTS):
            for r in range(2):
                k = rank[r]

                @pl.when(k >= 1)
                def _():
                    arrival(r, 0, f).wait_recv()
                    part[pl.ds(y, 1), :, chunk(f)] += crecv[t, r, pl.ds(0, 1), :, chunk(f)].astype(F32)

            for r in range(2):

                @pl.when(rank[r] <= 1)
                def _():
                    arrival(r, TRANSIT, f).wait_recv()

            own = part[pl.ds(y, 1), :, chunk(f)].reshape(ROWS, width)
            other = crecv[t, pl.ds(j // 2, 1), TRANSIT, :, chunk(f)].reshape(ROWS, width).astype(F32)
            first = half == 0
            low, high = jnp.where(first, own, other), jnp.where(first, other, own)
            rows = jnp.concatenate([low, high], axis=0).astype(BF16)
            rows = jnp.dot(backward, rows, preferred_element_type=F32)
            bsend[t, :, :, chunk(f)] = rows.reshape(XS, SLOTS, width).astype(BF16)
            for i in range(1, XS):
                target = lax.rem(x + i, XS)
                copy = remote(
                    bsend.at[t, target, :, chunk(f)], brecv.at[t, x, :, chunk(f)],
                    b_send.at[t, i - 1, f], b_recv.at[t, i - 1, f], at(target, y, core),
                )
                copy.start()
                remember(None, copy)
            brecv[t, pl.ds(x, 1), :, chunk(f)] = bsend[t, pl.ds(x, 1), :, chunk(f)]

    def finish(t, sources, mixes, keep):
        for f in range(PARTS):
            for i in range(1, XS):
                remote(
                    bsend.at[t, 0, :, chunk(f)], brecv.at[t, 0, :, chunk(f)],
                    b_send.at[t, i - 1, f], b_recv.at[t, i - 1, f], sibling,
                ).wait_recv()
            rows = brecv[t, :, :, chunk(f)].astype(F32).reshape(2 * ROWS, width).astype(BF16)
            for direction, (weight, undo) in enumerate(mixes):
                picked = jnp.dot(undo, rows, preferred_element_type=F32)
                result = sources[direction][:, chunk(f)].astype(F32) + weight * picked
                keep(direction, f, result.astype(BF16))

    last = pipes - 1
    edges = (pipe == 0, pipe == last)
    leaves = (pipe < last, pipe > 0)
    entering = (enter_up_ref, enter_down_ref)

    sources = (up_ref, down_ref)
    tables, picks = prepare(0, sources)
    send_rows(0, picks)

    for copy in own_weights:
        copy.wait()
    swaps = [
        (wgu.at[:, pl.ds(0, hid)], wgu.at[:, pl.ds(hid, hid)]),
        (wgu.at[:, pl.ds(2 * hid, hid)], wgu.at[:, pl.ds(3 * hid, hid)]),
        (wd.at[pl.ds(0, hid), :], wd.at[pl.ds(hid, hid), :]),
    ]
    swaps = [remote(src, dst, w_send.at[i], w_recv.at[i], sibling) for i, (src, dst) in enumerate(swaps)]
    for copy in swaps:
        copy.start()
        remember(None, copy)

    mixes = weigh(0, tables)
    spread(0)
    for copy in swaps:
        copy.wait_recv()
    experts(0)
    gather(0)

    def keep_moved(direction, f, value):
        moved_out[direction, :, chunk(f)] = value
        guarded(leaves[direction], lambda: remote(
            moved_out.at[direction, :, chunk(f)], moved.at[direction, :, chunk(f)],
            m_send.at[direction, f], m_recv.at[direction, f], shifts[direction],
        ))

    finish(0, sources, mixes, keep_moved)
    for direction in range(2):

        @pl.when(edges[direction])
        def _():
            moved[direction] = entering[direction][...]

        @pl.when(jnp.logical_not(edges[direction]))
        def _():
            for f in range(PARTS):
                remote(
                    moved_out.at[direction, :, chunk(f)], moved.at[direction, :, chunk(f)],
                    m_send.at[direction, f], m_recv.at[direction, f], shifts[direction],
                ).wait_recv()

    sources = (moved.at[0], moved.at[1])
    tables, picks = prepare(1, sources)
    send_rows(1, picks)
    mixes = weigh(1, tables)
    spread(1)
    experts(1)
    gather(1)

    outs = (up_out_ref, down_out_ref)

    def keep_out(direction, f, value):
        outs[direction][:, chunk(f)] = value

    finish(1, sources, mixes, keep_out)

    for condition, copy in sent:
        if condition is None:
            copy.wait_send()
        else:

            @pl.when(condition)
            def _():
                copy.wait_send()


def shards(pipes, up_state, down_state, enter_up, enter_down, up_route, down_route, gain, router, w_gate, w_up, w_down):
    features = up_state.shape[2]
    hid = w_down.shape[1]
    vmem = pl.BlockSpec(memory_space=pltpu.VMEM)
    hbm = pl.BlockSpec(memory_space=pl.ANY)
    dma = pltpu.SemaphoreType.DMA
    block = jax.ShapeDtypeStruct((ROWS, features), BF16)
    up_out, down_out = pl.pallas_call(
        functools.partial(kernel, pipes),
        out_shape=(block, block),
        in_specs=[vmem] * 8 + [hbm] * 3,
        out_specs=(vmem, vmem),
        scratch_shapes=[
            pltpu.VMEM((features, 4 * hid), BF16),
            pltpu.VMEM((2 * hid, features), BF16),
            pltpu.VMEM((2, ROWS, features), BF16),
            pltpu.VMEM((TICKS, XS, SLOTS, features), BF16),
            pltpu.VMEM((TICKS, XS, SLOTS, features), BF16),
            pltpu.VMEM((TICKS, ROWS, features), BF16),
            pltpu.VMEM((TICKS, YS, ROWS, features), BF16),
            pltpu.VMEM((TICKS, 2, ROWS, features), BF16),
            pltpu.VMEM((YS, ROWS, features), F32),
            pltpu.VMEM((TICKS, 2, REACH, ROWS, features), BF16),
            pltpu.VMEM((TICKS, 2, REACH + 1, ROWS, features), BF16),
            pltpu.VMEM((TICKS, XS, SLOTS, features), BF16),
            pltpu.VMEM((TICKS, XS, SLOTS, features), BF16),
            pltpu.VMEM((2, ROWS, features), BF16),
            pltpu.VMEM((2, ROWS, features), BF16),
            dma((3,)),
            dma((3,)),
            dma((3,)),
            dma((TICKS, XS - 1, PARTS)),
            dma((TICKS, XS - 1, PARTS)),
            dma((TICKS, 2, 6, PARTS)),
            dma((TICKS, 2, 6, PARTS)),
            dma((TICKS, 2, 6, PARTS)),
            dma((TICKS, 2, 6, PARTS)),
            dma((TICKS, XS - 1, PARTS)),
            dma((TICKS, XS - 1, PARTS)),
            dma((2, PARTS)),
            dma((2, PARTS)),
        ],
        compiler_params=pltpu.CompilerParams(
            collective_id=0, has_side_effects=True, vmem_limit_bytes=56 * 1024 * 1024
        ),
    )(
        up_state[0], down_state[0], enter_up, enter_down,
        up_route.reshape(TICKS, ROWS), down_route.reshape(TICKS, ROWS),
        gain, router[0].T, w_gate[0], w_up[0], w_down[0],
    )
    return up_out[None], down_out[None]


def solution(mesh):
    return jax.shard_map(
        functools.partial(shards, mesh.shape["pipe"]),
        mesh=mesh,
        in_specs=(
            P("pipe", "expert", None),
            P("pipe", "expert", None),
            P("expert", None),
            P("expert", None),
            P(None, "pipe", "expert", None),
            P(None, "pipe", "expert", None),
            P("pipe", None),
            P("pipe", None, None),
            P("pipe", None, "expert"),
            P("pipe", None, "expert"),
            P("pipe", "expert", None),
        ),
        out_specs=(P("pipe", "expert", None), P("pipe", "expert", None)),
        check_vma=False,
    )
```

time: 293 us -> 131 us (0.45)
  the two profiles are of different devices: /device:TPU:398 before, /device:TPU:30 now
where the time goes in v1:
time: 131 us
  Pallas kernels  128 us (98%)
  local copies, waits for them, and re-layouts  2.24 us (2%)
    pallas_call x1, Pallas kernels, shards(): pl.pallas_call(functools.partial(kernel, pipes), out_shape=(block, block)...  128 us

profile of v1, /device:TPU:30, one launch (start us, length us, event | category | flops | bytes accessed | tf_op | source)
XLA Modules:
  0.0 130.7 jit_solution(13494970109772752148)
XLA Ops:
  0.6 127.8 %shard_map.122 = (bf16[16,3584]{1,0:T(8,128)(2,1)}, bf16[16,3584]{1,0:T(8,128)(2,1)}) custom-call(bf16[16,3584]{1,0:T(8,128)(2,1)} %bitcast.17, bf16[16,3584]{1,0:T(8,128)(2,1)} %bitcast.18, bf16[16,3584]{1,0:T(8,128)(2,1)} %enter_up_ref.1, bf16[16,3584]{1,0:T(8,128)(2,1)} %enter_down_ref.1, s32[2,16]{1,0:T(2,128)} %bitcast.20, s32[2,16]{1,0:T(2,128)} %bitcast.21, ...), custom_call_target="tpu_custom_call" | custom-call | tf_op jit(solution)/shard_map/pallas_call | solution.py:422
  128.5 0.0 copy-start
  128.5 1.6 %copy.15 = bf16[1,16,3584]{2,1,0:T(8,128)(2,1)} copy(bf16[1,16,3584]{2,1,0:T(8,128)(2,1)} %bitcast.16) | data formatting | bytes 229376
  130.1 0.0 copy-done
  130.1 0.6 copy.16
Async XLA Ops:
  128.5 1.6 %copy-start = (bf16[16,3584]{1,0:T(8,128)(2,1)S(1)}, bf16[16,3584]{1,0:T(8,128)(2,1)}, u32[]{:S(2)}) copy-start(bf16[16,3584]{1,0:T(8,128)(2,1)} %get-tuple-element.5) | copy-start | bytes 344068

commit v2 on v0

v2 whole, which is shorter than its diff:
```python
import functools

import jax
import jax.numpy as jnp
from jax import lax
from jax.experimental import pallas as pl
from jax.experimental.pallas import tpu as pltpu
from jax.sharding import PartitionSpec as P

XS, YS, CORES = 4, 8, 2
HALF = YS // 2
TICKS = 2
ROWS = 16
PARTS = 2
SUB = 8
REACH = 5
TRANSIT = 5
norm_eps = 1e-06

MESH = pl.DeviceIdType.MESH
F32, BF16 = jnp.float32, jnp.bfloat16


def iota(shape, dim):
    return lax.broadcasted_iota(jnp.int32, shape, dim)


def turned(row):
    n = row.shape[1]
    eye = iota((n, n), 0) == iota((n, n), 1)
    return jnp.sum(jnp.where(eye, jnp.broadcast_to(row, (n, n)), 0.0), axis=1, keepdims=True)


def slots_of(route):
    n = route.shape[1]
    column = turned(route)
    earlier = iota((n, n), 0) < iota((n, n), 1)
    same = (jnp.broadcast_to(column, (n, n)) == jnp.broadcast_to(route, (n, n))) & earlier
    number = jnp.sum(jnp.where(same, 1.0, 0.0), axis=0, keepdims=True)
    return route * 2.0 + number


def packed(shape, dim):
    i = iota(shape, dim)
    return (i // SUB) * 4 + i % 4, (i // 4) % 2


def kernel(
    pipes,
    up_ref, down_ref, enter_up_ref, enter_down_ref, up_route_ref, down_route_ref,
    gain_ref, router_ref, w_gate_ref, w_up_ref, w_down_ref,
    out_ref,
    wgu, wd, cur, normed, xsend, xrecv, away, blocks, pass_on, part, csend, crecv, bsend, brecv, before, tables_out,
    tables_in, result,
    w_local, w_send, w_recv, in_sem, out_sem, x_send, x_recv, y_send, y_recv, c_send, c_recv, b_send, b_recv,
    m_send, m_recv,
):
    features = up_ref.shape[1]
    width = features // PARTS
    lanes = width // 2
    hid = w_down_ref.shape[0]
    pipe = lax.axis_index("pipe")
    place = lax.axis_index("expert")
    core = lax.rem(place, CORES)
    y = lax.rem(lax.div(place, CORES), YS)
    x = lax.div(place, CORES * YS)
    half = lax.div(y, HALF)
    j = lax.rem(y, HALF)

    def at(xx, yy, cc):
        return (pipe, (xx * YS + yy) * CORES + cc)

    def chunk(f):
        return pl.ds(pl.multiple_of(f * width, 128), width)

    def side(h):
        return pl.ds(h * lanes, lanes)

    def remote(src, dst, send, recv, device):
        return pltpu.make_async_remote_copy(
            src_ref=src, dst_ref=dst, send_sem=send, recv_sem=recv, device_id=device, device_id_type=MESH
        )

    sibling = at(x, y, 1 - core)
    nexts = (at(x, lax.rem(y + 1, YS), core), at(x, lax.rem(y + YS - 1, YS), core))
    columns = [lax.rem(x + i, XS) for i in range(XS)]
    neighbours = (lax.rem(pipe + 1, pipes), lax.rem(pipe + pipes - 1, pipes))
    edges = (pipe == 0, pipe == pipes - 1)
    leaves = (pipe < pipes - 1, pipe > 0)

    def beyond(g, i):
        return (neighbours[g], (columns[i] * YS + y) * CORES + core)

    def toward(r, d):
        return lax.rem(y + (d if r == 0 else YS - d), YS)

    rank = (j, HALF - 1 - j)

    def loads():
        for g, ref in enumerate((up_ref, down_ref)):
            for f in range(PARTS):
                yield pltpu.make_async_copy(ref.at[:, chunk(f)], cur.at[0, g, f], in_sem.at[0, g, f])

    def enters(g):
        ref = (enter_up_ref, enter_down_ref)[g]
        for f in range(PARTS):
            yield pltpu.make_async_copy(ref.at[:, chunk(f)], cur.at[1, g, f], in_sem.at[1, g, f])

    own_weights = [
        pltpu.make_async_copy(w_gate_ref, wgu.at[:, pl.ds(0, hid)], w_local.at[0]),
        pltpu.make_async_copy(w_up_ref, wgu.at[:, pl.ds(2 * hid, hid)], w_local.at[1]),
        pltpu.make_async_copy(w_down_ref, wd.at[pl.ds(0, hid), :], w_local.at[2]),
    ]
    for copy in loads():
        copy.start()
    for copy in own_weights:
        copy.start()
    for g in range(2):

        @pl.when(edges[g])
        def _():
            for copy in enters(g):
                copy.start()

    barrier = pltpu.get_barrier_semaphore()
    partners = [at(columns[i], y, core) for i in range(1, XS)] + [*nexts, sibling]
    partners += [beyond(g, i) for g in range(2) for i in range(XS)]
    for device in partners:
        pl.semaphore_signal(barrier, inc=1, device_id=device, device_id_type=MESH)

    swaps = [
        (wgu.at[:, pl.ds(0, hid)], wgu.at[:, pl.ds(hid, hid)]),
        (wgu.at[:, pl.ds(2 * hid, hid)], wgu.at[:, pl.ds(3 * hid, hid)]),
        (wd.at[pl.ds(0, hid), :], wd.at[pl.ds(hid, hid), :]),
    ]
    swaps = [remote(src, dst, w_send.at[i], w_recv.at[i], sibling) for i, (src, dst) in enumerate(swaps)]

    def x_copy(t, g, i, f):
        return remote(
            xsend.at[t, g, f, columns[i]], xrecv.at[t, g, f, x], x_send.at[t, g, i, f], x_recv.at[t, g, i, f],
            at(columns[i], y, core),
        )

    def b_copy(t, g, i, f):
        device = beyond(g, i) if t == 0 else at(columns[i], y, core)
        return remote(
            bsend.at[t, g, f, columns[i]], brecv.at[t, g, f, x], b_send.at[t, g, i, f], b_recv.at[t, g, i, f], device,
        )

    def y_copy(t, g, r, f, src, dst, slot):
        return remote(src, dst, y_send.at[t, g, r, slot, f], y_recv.at[t, g, r, slot, f], nexts[r])

    def c_copy(t, g, r, f, src, dst, out_slot, in_slot):
        return remote(src, dst, c_send.at[t, g, r, out_slot, f], c_recv.at[t, g, r, in_slot, f], nexts[r])

    def m_copies(g):
        yield remote(cur.at[0, g], before.at[g], m_send.at[g, 0], m_recv.at[g, 0], beyond(g, 0))
        yield remote(tables_out.at[g], tables_in.at[g], m_send.at[g, 1], m_recv.at[g, 1], beyond(g, 0))

    def out_copy(g, f):
        return pltpu.make_async_copy(result.at[g, f], out_ref.at[g, :, chunk(f)], out_sem.at[g, f])

    def spot_of(t, g):
        route = (up_route_ref, down_route_ref)[g][pl.ds(t, 1), :].astype(F32)
        return route, slots_of(route)

    def send_rows(t, g):
        squares = jnp.zeros((ROWS, width), F32)
        for f in range(PARTS):
            rows = cur[t, g, f].astype(F32)
            squares = squares + rows * rows
        scale = lax.rsqrt(jnp.sum(squares, axis=1, keepdims=True) / features + norm_eps)
        _, spot = spot_of(t, g)
        row, lane_half = packed((2 * ROWS, ROWS), 0)
        picks = [
            ((row.astype(F32) == jnp.broadcast_to(spot, (2 * ROWS, ROWS))) & (lane_half == h)).astype(BF16)
            for h in range(2)
        ]
        if (t, g) == (0, 0):
            pl.semaphore_wait(barrier, len(partners))

        @pl.loop(0, PARTS)
        def _(f):
            own = (cur[t, g, f].astype(F32) * scale * gain_ref[:, chunk(f)]).astype(BF16)
            normed[g, f] = own
            rows = jnp.dot(picks[0], own[:, :lanes], preferred_element_type=F32) + jnp.dot(
                picks[1], own[:, lanes:], preferred_element_type=F32
            )
            xsend[t, g, f] = rows.reshape(XS, SUB, lanes).astype(BF16)
            for i in range(1, XS):
                x_copy(t, g, i, f).start()
            xrecv[t, g, f, pl.ds(x, 1)] = xsend[t, g, f, pl.ds(x, 1)]

    kept = {}

    def weigh(t, g):
        route, spot = spot_of(t, g)
        count = router_ref.shape[0]
        logits = jnp.zeros((count, ROWS), F32)
        for f in range(PARTS):
            logits = logits + lax.dot_general(
                router_ref[:, f * width : (f + 1) * width], normed[g, f], (((1,), (1,)), ((), ())),
                preferred_element_type=F32,
            )
        affinity = jax.nn.sigmoid(logits)
        hit = iota((count, ROWS), 0).astype(F32) == jnp.broadcast_to(route, (count, ROWS))
        weight = turned(jnp.sum(jnp.where(hit, affinity, 0.0), axis=0, keepdims=True))
        if t == 0:
            tables_out[g, 0] = jnp.broadcast_to(weight, (ROWS, 128))
            tables_out[g, 1] = jnp.broadcast_to(turned(spot), (ROWS, 128))

            @pl.when(leaves[g])
            def _():
                for copy in m_copies(g):
                    copy.start()
        else:
            kept[g] = (weight, turned(spot))

    def own_blocks(t, g):
        b, a = iota((ROWS, 2 * ROWS), 0), iota((ROWS, 2 * ROWS), 1)
        want = ((b // 2) % XS) * SUB + (b // SUB) * 2 + b % 2
        maps = [(want + 4 * h == a).astype(BF16) for h in range(2)]

        @pl.loop(0, PARTS)
        def _(f):
            for i in range(1, XS):
                x_copy(t, g, i, f).wait_recv()
            rows = xrecv[t, g, f].astype(F32).reshape(2 * ROWS, lanes).astype(BF16)
            first = half == 0
            for h in range(2):
                both = jnp.dot(maps[h], rows, preferred_element_type=F32)
                low, high = both[:SUB], both[SUB:]
                blocks[t, g, f, pl.ds(y, 1), :, side(h)] = jnp.where(first, low, high).astype(BF16)[None]
                away[t, g, f, :, side(h)] = jnp.where(first, high, low).astype(BF16)
            for r in range(2):
                k = rank[r]

                @pl.when(k == HALF - 2)
                def _():
                    y_copy(t, g, r, f, away.at[t, g, f], pass_on.at[t, g, r, f], TRANSIT).start()

                @pl.when(k == HALF - 1)
                def _():
                    y_copy(t, g, r, f, away.at[t, g, f], blocks.at[t, g, f, y], 0).start()

                @pl.when(k < HALF - 1)
                def _():
                    y_copy(t, g, r, f, blocks.at[t, g, f, y], blocks.at[t, g, f, y], 0).start()

    def relay(t, g, d):
        if d == 0:

            @pl.loop(0, PARTS)
            def _(f):
                for r in range(2):

                    @pl.when(rank[r] == HALF - 1)
                    def _():
                        slot = toward(1 - r, 1)
                        y_copy(t, g, r, f, pass_on.at[t, g, r, f], pass_on.at[t, g, r, f], TRANSIT).wait_recv()
                        y_copy(t, g, r, f, pass_on.at[t, g, r, f], blocks.at[t, g, f, slot], 1).start()

            return

        @pl.loop(0, PARTS)
        def _(f):
            for r in range(2):
                k = rank[r]
                slot = toward(1 - r, d)

                @pl.when(d <= k + 2)
                def _():
                    y_copy(t, g, r, f, blocks.at[t, g, f, slot], blocks.at[t, g, f, slot], d - 1).wait_recv()

                if d < REACH:

                    @pl.when((d <= k + 2) & (k < HALF - 1))
                    def _():
                        y_copy(t, g, r, f, blocks.at[t, g, f, slot], blocks.at[t, g, f, slot], d).start()

    def experts(t, g):
        total = jnp.zeros((YS * SUB, 4 * hid), F32)
        for f in range(PARTS):
            total = total + jnp.dot(
                blocks[t, g, f].astype(F32).reshape(YS * SUB, width).astype(BF16),
                wgu[f * width : (f + 1) * width, :],
                preferred_element_type=F32,
            )
        gate, up = total[:, : 2 * hid], total[:, 2 * hid :]
        hidden = (gate / (1.0 + jnp.exp(-gate)) * up).astype(BF16)
        for f in range(PARTS):
            piece = jnp.dot(hidden, wd[:, f * width : (f + 1) * width], preferred_element_type=F32)
            part[g, f] = piece.reshape(YS, SUB, width)

    def arrival(t, g, r, slot, f):
        return c_copy(t, g, r, f, csend.at[t, g, r, f, 0], crecv.at[t, g, r, f, slot], 0, slot)

    def gather(t, g, d):
        if d == 0:

            @pl.loop(0, PARTS)
            def _(f):
                for r in range(2):

                    @pl.when(rank[r] == 0)
                    def _():
                        arrival(t, g, r, 4, f).wait_recv()
                        c_copy(
                            t, g, r, f, crecv.at[t, g, r, f, 4], crecv.at[t, g, r, f, TRANSIT], TRANSIT, TRANSIT
                        ).start()

            return

        @pl.loop(0, PARTS)
        def _(f):
            for r in range(2):
                k = rank[r]
                slot = toward(r, d)

                @pl.when(k == 0)
                def _():
                    csend[t, g, r, f, d - 1] = part[g, f, pl.ds(slot, 1)].reshape(SUB, width).astype(BF16)

                if d < REACH:

                    @pl.when((k >= 1) & (d <= REACH - k))
                    def _():
                        arrival(t, g, r, d, f).wait_recv()
                        both = part[g, f, pl.ds(slot, 1)].reshape(SUB, width) + crecv[t, g, r, f, d].astype(F32)
                        csend[t, g, r, f, d - 1] = both.astype(BF16)

                @pl.when((d <= REACH - k) & (k < HALF - 1))
                def _():
                    c_copy(
                        t, g, r, f, csend.at[t, g, r, f, d - 1], crecv.at[t, g, r, f, d - 1], d - 1, d - 1
                    ).start()

                if d <= 2:

                    @pl.when(k == HALF - 1)
                    def _():
                        c_copy(
                            t, g, r, f, csend.at[t, g, r, f, d - 1], crecv.at[t, g, r, f, 6 - d], d - 1, 6 - d
                        ).start()

    def send_back(t, g):
        a, b = iota((2 * ROWS, ROWS), 0), iota((2 * ROWS, ROWS), 1)
        want = ((b // 2) % XS) * SUB + (b // SUB) * 2 + b % 2
        maps = [(want + 4 * h == a).astype(BF16) for h in range(2)]

        @pl.loop(0, PARTS)
        def _(f):
            for r in range(2):

                @pl.when(rank[r] >= 1)
                def _():
                    arrival(t, g, r, 0, f).wait_recv()
                    part[g, f, pl.ds(y, 1)] += crecv[t, g, r, f, pl.ds(0, 1)].astype(F32)

            for r in range(2):

                @pl.when(rank[r] <= 1)
                def _():
                    arrival(t, g, r, TRANSIT, f).wait_recv()

            own = part[g, f, pl.ds(y, 1)].reshape(SUB, width)
            other = crecv[t, g, pl.ds(lax.div(j, 2), 1), f, TRANSIT].reshape(SUB, width).astype(F32)
            first = half == 0
            rows = jnp.concatenate([jnp.where(first, own, other), jnp.where(first, other, own)], axis=0).astype(BF16)
            rows = jnp.dot(maps[0], rows[:, :lanes], preferred_element_type=F32) + jnp.dot(
                maps[1], rows[:, lanes:], preferred_element_type=F32
            )
            bsend[t, g, f] = rows.reshape(XS, SUB, lanes).astype(BF16)
            if t == 0:

                @pl.when(leaves[g])
                def _():
                    for i in range(XS):
                        b_copy(t, g, i, f).start()
            else:
                for i in range(1, XS):
                    b_copy(t, g, i, f).start()
                brecv[t, g, f, pl.ds(x, 1)] = bsend[t, g, f, pl.ds(x, 1)]

    def settle(t, g):
        row, lane_half = packed((ROWS, 2 * ROWS), 1)

        def mixed(weight, spot, keep, rows_of):
            undo = [
                ((row.astype(F32) == jnp.broadcast_to(spot, (ROWS, 2 * ROWS))) & (lane_half == h)).astype(BF16)
                for h in range(2)
            ]

            @pl.loop(0, PARTS)
            def _(f):
                for i in range(0 if t == 0 else 1, XS):
                    b_copy(t, g, i, f).wait_recv()
                rows = brecv[t, g, f].astype(F32).reshape(2 * ROWS, lanes).astype(BF16)
                for h in range(2):
                    picked = jnp.dot(undo[h], rows, preferred_element_type=F32)
                    keep(f, h, (rows_of(f, h).astype(F32) + weight * picked).astype(BF16))

        if t == 0:

            @pl.when(edges[g])
            def _():
                for copy in enters(g):
                    copy.wait()

            @pl.when(jnp.logical_not(edges[g]))
            def _():
                for copy in m_copies(g):
                    copy.wait_recv()

                def keep(f, h, value):
                    cur[1, g, f, :, side(h)] = value

                mixed(
                    tables_in[g, 0][:, :1], tables_in[g, 1][:, :1], keep, lambda f, h: before[g, f, :, side(h)]
                )

        else:

            def keep(f, h, value):
                result[g, f, :, side(h)] = value

            mixed(*kept[g], keep, lambda f, h: cur[1, g, f, :, side(h)])
            for f in range(PARTS):
                out_copy(g, f).start()

    def start_swaps():
        for copy in own_weights:
            copy.wait()
        for copy in swaps:
            copy.start()

    def end_swaps():
        for copy in swaps:
            copy.wait_recv()

    for copy in loads():
        copy.wait()

    def both(task, *rest):
        for g in range(2):
            task(rest[0], g, *rest[1:])

    for t in range(TICKS):
        both(send_rows, t)
        if t == 0:
            start_swaps()
        both(own_blocks, t)
        for d in range(REACH + 1):
            both(relay, t, d)
        if t == 0:
            end_swaps()
        both(experts, t)
        for d in range(REACH, -1, -1):
            both(gather, t, d)
            if d == REACH:
                both(weigh, t)
        both(send_back, t)
        both(settle, t)

    for copy in swaps:
        copy.wait_send()
    for g in range(2):

        @pl.when(leaves[g])
        def _():
            for copy in m_copies(g):
                copy.wait_send()

            @pl.loop(0, PARTS)
            def _(f):
                for i in range(XS):
                    b_copy(0, g, i, f).wait_send()

    @pl.loop(0, 2)
    def _(g):
        @pl.loop(0, PARTS)
        def _(f):
            for i in range(1, XS):
                remote(
                    bsend.at[1, g, f, 0], brecv.at[1, g, f, 0], b_send.at[1, g, i, f], b_recv.at[1, g, i, f], sibling
                ).wait_send()

            @pl.loop(0, TICKS)
            def _(t):
                for i in range(1, XS):
                    x_copy(t, g, i, f).wait_send()
                for r in range(2):
                    k = rank[r]

                    @pl.loop(0, TRANSIT + 1)
                    def _(slot):
                        spreads = jnp.where(k == HALF - 1, slot <= 1, (slot <= k + 2) & (slot < TRANSIT))

                        @pl.when(spreads | ((slot == TRANSIT) & (k == HALF - 2)))
                        def _():
                            y_copy(t, g, r, f, away.at[t, g, f], pass_on.at[t, g, r, f], slot).wait_send()

                        @pl.when((slot < REACH - k) | ((slot == TRANSIT) & (k == 0)))
                        def _():
                            c_copy(
                                t, g, r, f, csend.at[t, g, r, f, 0], crecv.at[t, g, r, f, 0], slot, 0
                            ).wait_send()

    for g in range(2):
        for f in range(PARTS):
            out_copy(g, f).wait()


def shards(pipes, up_state, down_state, enter_up, enter_down, up_route, down_route, gain, router, w_gate, w_up, w_down):
    features = up_state.shape[2]
    hid = w_down.shape[1]
    vmem = pl.BlockSpec(memory_space=pltpu.VMEM)
    hbm = pl.BlockSpec(memory_space=pl.ANY)
    dma = pltpu.SemaphoreType.DMA
    width = features // PARTS
    out = pl.pallas_call(
        functools.partial(kernel, pipes),
        out_shape=jax.ShapeDtypeStruct((2, ROWS, features), BF16),
        in_specs=[hbm] * 4 + [vmem] * 4 + [hbm] * 3,
        out_specs=hbm,
        scratch_shapes=[
            pltpu.VMEM((features, 4 * hid), BF16),
            pltpu.VMEM((2 * hid, features), BF16),
            pltpu.VMEM((TICKS, 2, PARTS, ROWS, width), BF16),
            pltpu.VMEM((2, PARTS, ROWS, width), BF16),
            pltpu.VMEM((TICKS, 2, PARTS, XS, SUB, width // 2), BF16),
            pltpu.VMEM((TICKS, 2, PARTS, XS, SUB, width // 2), BF16),
            pltpu.VMEM((TICKS, 2, PARTS, SUB, width), BF16),
            pltpu.VMEM((TICKS, 2, PARTS, YS, SUB, width), BF16),
            pltpu.VMEM((TICKS, 2, 2, PARTS, SUB, width), BF16),
            pltpu.VMEM((2, PARTS, YS, SUB, width), F32),
            pltpu.VMEM((TICKS, 2, 2, PARTS, REACH, SUB, width), BF16),
            pltpu.VMEM((TICKS, 2, 2, PARTS, REACH + 1, SUB, width), BF16),
            pltpu.VMEM((TICKS, 2, PARTS, XS, SUB, width // 2), BF16),
            pltpu.VMEM((TICKS, 2, PARTS, XS, SUB, width // 2), BF16),
            pltpu.VMEM((2, PARTS, ROWS, width), BF16),
            pltpu.VMEM((2, 2, ROWS, 128), F32),
            pltpu.VMEM((2, 2, ROWS, 128), F32),
            pltpu.VMEM((2, PARTS, ROWS, width), BF16),
            dma((3,)),
            dma((3,)),
            dma((3,)),
            dma((2, 2, PARTS)),
            dma((2, PARTS)),
            dma((TICKS, 2, XS, PARTS)),
            dma((TICKS, 2, XS, PARTS)),
            dma((TICKS, 2, 2, TRANSIT + 1, PARTS)),
            dma((TICKS, 2, 2, TRANSIT + 1, PARTS)),
            dma((TICKS, 2, 2, TRANSIT + 1, PARTS)),
            dma((TICKS, 2, 2, TRANSIT + 1, PARTS)),
            dma((TICKS, 2, XS, PARTS)),
            dma((TICKS, 2, XS, PARTS)),
            dma((2, 2)),
            dma((2, 2)),
        ],
        compiler_params=pltpu.CompilerParams(
            collective_id=0, has_side_effects=True, vmem_limit_bytes=56 * 1024 * 1024
        ),
    )(
        up_state[0], down_state[0], enter_up, enter_down,
        up_route.reshape(TICKS, ROWS), down_route.reshape(TICKS, ROWS),
        gain, router[0].T, w_gate[0], w_up[0], w_down[0],
    )
    return out[:1], out[1:]


def solution(mesh):
    return jax.shard_map(
        functools.partial(shards, mesh.shape["pipe"]),
        mesh=mesh,
        in_specs=(
            P("pipe", "expert", None),
            P("pipe", "expert", None),
            P("expert", None),
            P("expert", None),
            P(None, "pipe", "expert", None),
            P(None, "pipe", "expert", None),
            P("pipe", None),
            P("pipe", None, None),
            P("pipe", None, "expert"),
            P("pipe", None, "expert"),
            P("pipe", "expert", None),
        ),
        out_specs=(P("pipe", "expert", None), P("pipe", "expert", None)),
        check_vma=False,
    )
```

time: 293 us -> 128 us (0.44)
  the two profiles are of different devices: /device:TPU:398 before, /device:TPU:30 now
where the time goes in v2:
time: 128 us; the launch traced here: 127 us
  Pallas kernels  125 us (98%)
  local copies, waits for them, and re-layouts  1.65 us (1%)
    pallas_call x1, Pallas kernels, shards(): pl.pallas_call(functools.partial(kernel, pipes), out_shape=jax.ShapeDtype...  125 us

profile of v2, /device:TPU:30, one launch (start us, length us, event | category | flops | bytes accessed | tf_op | source)
XLA Modules:
  0.0 127.3 jit_solution(15539279063936871814)
XLA Ops:
  0.6 125.0 %shard_map.122 = bf16[2,16,3584]{2,1,0:T(8,128)(2,1)} custom-call(bf16[16,3584]{1,0:T(8,128)(2,1)} %bitcast.13, bf16[16,3584]{1,0:T(8,128)(2,1)} %bitcast.14, bf16[16,3584]{1,0:T(8,128)(2,1)} %enter_up_ref.1, bf16[16,3584]{1,0:T(8,128)(2,1)} %enter_down_ref.1, s32[2,16]{1,0:T(2,128)} %bitcast.16, s32[2,16]{1,0:T(2,128)} %bitcast.17, f32[1,3584]{1,0:T(1,128)} %gain_ref.1, ...), custom_call_target="tpu_custom_call" | custom-call | tf_op jit(solution)/shard_map/pallas_call | solution.py:521
  125.6 1.7 %fusion = (bf16[1,16,3584]{2,1,0:T(8,128)(2,1)}, bf16[1,16,3584]{2,1,0:T(8,128)(2,1)}) fusion(bf16[2,16,3584]{2,1,0:T(8,128)(2,1)} %shard_map.122), kind=kLoop, calls=%fused_computation | loop fusion | bytes 458752 | tf_op jit(solution)/shard_map/slice | solution.py:569

commit v3 on v2

--- a/solution.py
+++ b/solution.py
@@ -278,19 +278,21 @@
                     def _():
                         y_copy(t, g, r, f, blocks.at[t, g, f, slot], blocks.at[t, g, f, slot], d).start()
 
-    def experts(t, g):
-        total = jnp.zeros((YS * SUB, 4 * hid), F32)
-        for f in range(PARTS):
+    def experts(t):
+        count = YS * SUB
+        total = jnp.zeros((2 * count, 4 * hid), F32)
+        for f in range(PARTS):
+            rows = [blocks[t, g, f].astype(F32).reshape(count, width) for g in range(2)]
             total = total + jnp.dot(
-                blocks[t, g, f].astype(F32).reshape(YS * SUB, width).astype(BF16),
-                wgu[f * width : (f + 1) * width, :],
+                jnp.concatenate(rows, axis=0).astype(BF16), wgu[f * width : (f + 1) * width, :],
                 preferred_element_type=F32,
             )
         gate, up = total[:, : 2 * hid], total[:, 2 * hid :]
         hidden = (gate / (1.0 + jnp.exp(-gate)) * up).astype(BF16)
         for f in range(PARTS):
             piece = jnp.dot(hidden, wd[:, f * width : (f + 1) * width], preferred_element_type=F32)
-            part[g, f] = piece.reshape(YS, SUB, width)
+            for g in range(2):
+                part[g, f] = piece[g * count : (g + 1) * count].reshape(YS, SUB, width)
 
     def arrival(t, g, r, slot, f):
         return c_copy(t, g, r, f, csend.at[t, g, r, f, 0], crecv.at[t, g, r, f, slot], 0, slot)
@@ -441,6 +443,46 @@
     for copy in loads():
         copy.wait()
 
+    def drain():
+        for copy in swaps:
+            copy.wait_send()
+        for g in range(2):
+
+            @pl.when(leaves[g])
+            def _():
+                for copy in m_copies(g):
+                    copy.wait_send()
+
+                @pl.loop(0, PARTS)
+                def _(f):
+                    for i in range(XS):
+                        b_copy(0, g, i, f).wait_send()
+
+        @pl.loop(0, 2)
+        def _(g):
+            @pl.loop(0, PARTS)
+            def _(f):
+                @pl.loop(0, TICKS)
+                def _(t):
+                    for i in range(1, XS):
+                        x_copy(t, g, i, f).wait_send()
+                    for r in range(2):
+                        k = rank[r]
+
+                        @pl.loop(0, TRANSIT + 1)
+                        def _(slot):
+                            spreads = jnp.where(k == HALF - 1, slot <= 1, (slot <= k + 2) & (slot < TRANSIT))
+
+                            @pl.when(spreads | ((slot == TRANSIT) & (k == HALF - 2)))
+                            def _():
+                                y_copy(t, g, r, f, away.at[t, g, f], pass_on.at[t, g, r, f], slot).wait_send()
+
+                            @pl.when((slot < REACH - k) | ((slot == TRANSIT) & (k == 0)))
+                            def _():
+                                c_copy(
+                                    t, g, r, f, csend.at[t, g, r, f, 0], crecv.at[t, g, r, f, 0], slot, 0
+                                ).wait_send()
+
     def both(task, *rest):
         for g in range(2):
             task(rest[0], g, *rest[1:])
@@ -454,58 +496,20 @@
             both(relay, t, d)
         if t == 0:
             end_swaps()
-        both(experts, t)
+        experts(t)
         for d in range(REACH, -1, -1):
             both(gather, t, d)
             if d == REACH:
                 both(weigh, t)
         both(send_back, t)
+        if t == TICKS - 1:
+            drain()
         both(settle, t)
 
-    for copy in swaps:
-        copy.wait_send()
     for g in range(2):
-
-        @pl.when(leaves[g])
-        def _():
-            for copy in m_copies(g):
-                copy.wait_send()
-
-            @pl.loop(0, PARTS)
-            def _(f):
-                for i in range(XS):
-                    b_copy(0, g, i, f).wait_send()
-
-    @pl.loop(0, 2)
-    def _(g):
-        @pl.loop(0, PARTS)
-        def _(f):
+        for f in range(PARTS):
             for i in range(1, XS):
-                remote(
-                    bsend.at[1, g, f, 0], brecv.at[1, g, f, 0], b_send.at[1, g, i, f], b_recv.at[1, g, i, f], sibling
-                ).wait_send()
-
-            @pl.loop(0, TICKS)
-            def _(t):
-                for i in range(1, XS):
-                    x_copy(t, g, i, f).wait_send()
-                for r in range(2):
-                    k = rank[r]
-
-                    @pl.loop(0, TRANSIT + 1)
-                    def _(slot):
-                        spreads = jnp.where(k == HALF - 1, slot <= 1, (slot <= k + 2) & (slot < TRANSIT))
-
-                        @pl.when(spreads | ((slot == TRANSIT) & (k == HALF - 2)))
-                        def _():
-                            y_copy(t, g, r, f, away.at[t, g, f], pass_on.at[t, g, r, f], slot).wait_send()
-
-                        @pl.when((slot < REACH - k) | ((slot == TRANSIT) & (k == 0)))
-                        def _():
-                            c_copy(
-                                t, g, r, f, csend.at[t, g, r, f, 0], crecv.at[t, g, r, f, 0], slot, 0
-                            ).wait_send()
-
+                b_copy(1, g, i, f).wait_send()
     for g in range(2):
         for f in range(PARTS):
             out_copy(g, f).wait()

time: 128 us -> 125 us (0.977)
  Pallas kernels: 125 us -> 122 us
    pallas_call x1, Pallas kernels: 125 us -> 122 us  [shards(): pl.pallas_call(functools.partial(kernel, pipes), out_shape=jax.ShapeDtype...]
where the time goes in v3:
time: 125 us; the launch traced here: 124 us
  Pallas kernels  122 us (98%)
  local copies, waits for them, and re-layouts  1.65 us (1%)
    pallas_call x1, Pallas kernels, shards(): pl.pallas_call(functools.partial(kernel, pipes), out_shape=jax.ShapeDtype...  122 us

profile of v3, /device:TPU:30, one launch (start us, length us, event | category | flops | bytes accessed | tf_op | source)
XLA Modules:
  0.0 124.4 jit_solution(4237835545074115426)
XLA Ops:
  0.6 122.1 %shard_map.122 = bf16[2,16,3584]{2,1,0:T(8,128)(2,1)} custom-call(bf16[16,3584]{1,0:T(8,128)(2,1)} %bitcast.13, bf16[16,3584]{1,0:T(8,128)(2,1)} %bitcast.14, bf16[16,3584]{1,0:T(8,128)(2,1)} %enter_up_ref.1, bf16[16,3584]{1,0:T(8,128)(2,1)} %enter_down_ref.1, s32[2,16]{1,0:T(2,128)} %bitcast.16, s32[2,16]{1,0:T(2,128)} %bitcast.17, f32[1,3584]{1,0:T(1,128)} %gain_ref.1, ...), custom_call_target="tpu_custom_call" | custom-call | tf_op jit(solution)/shard_map/pallas_call | solution.py:525
  122.8 1.7 %fusion = (bf16[1,16,3584]{2,1,0:T(8,128)(2,1)}, bf16[1,16,3584]{2,1,0:T(8,128)(2,1)}) fusion(bf16[2,16,3584]{2,1,0:T(8,128)(2,1)} %shard_map.122), kind=kLoop, calls=%fused_computation | loop fusion | bytes 458752 | tf_op jit(solution)/shard_map/slice | solution.py:573
